TPU v7x, 256 devices: a whole 4x4x8 slice. The times are simulated.
256 devices in a mesh: mp: 4 (over z_lo, core), fsdp: 16 (over y, x), dp: 4 (over z_hi).
Axes of the slice: x: 4, y: 4, z: 8 (z_hi: 4, z_lo: 2; z = z_hi * 2 + z_lo), core: 2. Of those that a mesh axis runs over, the one named last changes fastest.
Arguments:
- gen_noise: float32 [4, 4096, 128], P('dp', 'fsdp'), may hold values from -6 to 6
- renoise: float32 [4, 4096, 128], P('dp', 'fsdp'), may hold values from -120 to 120
- gen_step: int32 [4], P('dp'), may hold values from 250 to 999
- renoise_step: int32 [4], P('dp'), may hold values from 20 to 979
- text_pooled: bfloat16 [4, 768], P('dp'), may hold values from -6 to 6
- embed: bfloat16 [3, 64, 3072], replicated, may hold values from -0.75 to 0.75
- mod_weight: bfloat16 [3, 1024, 6144], P(None, None, 'fsdp'), may hold values from -0.1875 to 0.1875
- proj_weight: bfloat16 [3, 3072, 3072], P(None, 'fsdp', 'mp'), may hold values from -0.109375 to 0.109375
- unembed: bfloat16 [3, 64, 3072], P(None, None, 'mp'), may hold values from -0.109375 to 0.109375
Outputs:
- gen_grad: float32 [3072, 3072], P('fsdp', 'mp')
- score_gap: float32 [4, 4096, 128], P('dp', 'fsdp')
All inputs are finite; a program needn't handle non-finite values. Where the computation divides by a largest or mean magnitude, that divisor is 1e-20 or more.
Results may differ from a plain program's by a relative error of at most 0.03.
Values may be sent and summed in bfloat16 or wider, within the bound.
A program may use at most 128 MiB of HBM per device.

v0:
```python
import math
import jax
import jax.numpy as jnp
from jax import lax
from jax.sharding import PartitionSpec as P

D = 3072
CH = 64
TEMB = 256
GUIDANCE = 3.5
EPS_NORM = 1e-06
EPS_GAP = 1e-05


def sinusoid(timesteps):
    half_size = TEMB // 2
    frequency = jnp.exp(-math.log(10000.0) * jnp.arange(half_size, dtype=jnp.float32) / half_size)
    angles = timesteps.astype(jnp.float32)[:, None] * frequency[None, :]
    return jnp.concatenate([jnp.cos(angles), jnp.sin(angles)], axis=1)


def condition(timesteps, pooled):
    joined = jnp.concatenate([sinusoid(timesteps), pooled.astype(jnp.float32)], axis=1)
    return jax.nn.silu(joined).astype(jnp.bfloat16)


def normalize(values):
    average = jnp.mean(values, axis=1, keepdims=True)
    centred = values - average
    variance = jnp.mean(centred * centred, axis=1, keepdims=True)
    return centred * lax.rsqrt(variance + EPS_NORM)


def modulate(normed, modulation):
    return (normed * (1.0 + modulation[D:]) + modulation[:D]).astype(jnp.bfloat16)


def unembed_part(residual_sum, out_weight):
    return lax.dot_general(
        residual_sum.astype(jnp.bfloat16),
        out_weight,
        (((1,), (1,)), ((), ())),
        preferred_element_type=jnp.float32,
    )


def row_product(hidden, weight_piece):
    return jnp.dot(hidden, weight_piece, preferred_element_type=jnp.float32)


def body(
    gen_noise, renoise, gen_step, renoise_step, text_pooled, embed, mod_weight, proj_weight, unembed
):
    quarter = proj_weight.shape[2]
    col_start = lax.axis_index("mp") * quarter
    blank_text = jnp.zeros_like(text_pooled)
    noisy_vec = condition(renoise_step, text_pooled)
    local_mod = jnp.concatenate(
        [
            jnp.dot(
                condition(gen_step, text_pooled), mod_weight[0], preferred_element_type=jnp.float32
            ),
            jnp.dot(noisy_vec, mod_weight[1], preferred_element_type=jnp.float32),
            jnp.dot(
                condition(renoise_step, blank_text),
                mod_weight[1],
                preferred_element_type=jnp.float32,
            ),
            jnp.dot(noisy_vec, mod_weight[2], preferred_element_type=jnp.float32),
        ],
        axis=0,
    )
    modulation = lax.all_gather(local_mod, "fsdp", axis=1, tiled=True)
    latent = gen_noise[0].reshape(-1, CH)
    latent_bf = latent.astype(jnp.bfloat16)
    token_rows = latent.shape[0]
    embedded = jnp.dot(latent_bf, embed[0], preferred_element_type=jnp.float32)
    gen_hidden = modulate(normalize(embedded), modulation[0])
    gen_part = row_product(gen_hidden, lax.all_gather(proj_weight[0], "fsdp", axis=0, tiled=True))
    gen_cols = lax.dynamic_slice_in_dim(embedded, col_start, quarter, 1)
    clean_part = unembed_part(gen_cols + gen_part, unembed[0]).reshape(-1, 2 * CH)
    clean_lat = lax.psum(clean_part, "mp")
    noise_level = renoise_step[0].astype(jnp.float32) / 1000.0
    noisy_lat = (1.0 - noise_level) * clean_lat + noise_level * renoise[0]
    noisy_bf = noisy_lat.reshape(-1, CH).astype(jnp.bfloat16)
    teacher_in = jnp.dot(noisy_bf, embed[1], preferred_element_type=jnp.float32)
    teacher_norm = normalize(teacher_in)
    cond_hidden = modulate(teacher_norm, modulation[1])
    blank_hidden = modulate(teacher_norm, modulation[2])
    fake_in = jnp.dot(noisy_bf, embed[2], preferred_element_type=jnp.float32)
    fake_hidden = modulate(normalize(fake_in), modulation[3])
    pieces = (
        lax.all_gather(proj_weight[1], "fsdp", axis=0, tiled=True),
        lax.all_gather(proj_weight[2], "fsdp", axis=0, tiled=True),
    )
    cond_part = row_product(cond_hidden, pieces[0])
    blank_part = row_product(blank_hidden, pieces[0])
    fake_part = row_product(fake_hidden, pieces[1])
    teacher_cols = lax.dynamic_slice_in_dim(teacher_in, col_start, quarter, 1)
    fake_cols = lax.dynamic_slice_in_dim(fake_in, col_start, quarter, 1)
    cond_out, blank_out, fake_out = (
        lax.psum(
            unembed_part(teacher_cols + cond_part, unembed[1])
            .reshape(-1, 2 * CH)
            .astype(jnp.bfloat16),
            "mp",
        ).astype(jnp.float32),
        lax.psum(
            unembed_part(teacher_cols + blank_part, unembed[1])
            .reshape(-1, 2 * CH)
            .astype(jnp.bfloat16),
            "mp",
        ).astype(jnp.float32),
        lax.psum(
            unembed_part(fake_cols + fake_part, unembed[2])
            .reshape(-1, 2 * CH)
            .astype(jnp.bfloat16),
            "mp",
        ).astype(jnp.float32),
    )
    real_pred = noisy_lat - noise_level * (blank_out + GUIDANCE * (cond_out - blank_out))
    fake_pred = noisy_lat - noise_level * fake_out
    seq_len = token_rows * lax.axis_size("fsdp")
    gap_total = lax.psum(jnp.sum(jnp.abs(clean_lat - real_pred)), "fsdp")
    gap_scale = gap_total / (seq_len * CH) + EPS_GAP
    score_gap = (fake_pred - real_pred) / gap_scale
    all_tokens = seq_len * lax.axis_size("dp")
    cotangent = (score_gap / math.sqrt(all_tokens)).astype(jnp.bfloat16).reshape(-1, CH)
    upstream = jnp.dot(cotangent, unembed[0], preferred_element_type=jnp.float32).astype(
        jnp.bfloat16
    )
    row_terms = lax.psum_scatter(
        lax.dot_general(
            gen_hidden, upstream, (((0,), (0,)), ((), ())), preferred_element_type=jnp.float32
        ).astype(jnp.bfloat16),
        "fsdp",
        scatter_dimension=0,
        tiled=True,
    )
    gen_grad = lax.psum(row_terms, "dp").astype(jnp.float32)
    return (gen_grad, score_gap[None])


def solution(mesh):
    return jax.shard_map(
        body,
        mesh=mesh,
        in_specs=(
            P("dp", "fsdp", None),
            P("dp", "fsdp", None),
            P("dp"),
            P("dp"),
            P("dp", None),
            P(),
            P(None, None, "fsdp"),
            P(None, "fsdp", "mp"),
            P(None, None, "mp"),
        ),
        out_specs=(P("fsdp", "mp"), P("dp", "fsdp", None)),
        check_vma=False,
    )
```

profile of v0, /device:TPU:2, one launch (start us, length us, event | category | flops | bytes accessed | tf_op | source)
XLA Modules:
  0.0 498.5 jit_solution(18427168380381059458)
XLA Ops:
  7.2 2.1 fusion.104
  9.4 0.9 convert_element_type.109
  10.3 0.1 convert_element_type.110
  11.8 0.7 convert_reduce_fusion
  12.6 1.3 fusion.49
  13.9 1.3 fusion.53
  15.2 1.3 fusion.51
  16.6 1.3 fusion.55
  18.0 23.6 %all_gather.12 = f32[4,6144]{1,0:T(4,128)S(1)} all-gather(f32[4,384]{1,0:T(4,128)S(1)} %pad_maximum_fusion), channel_id=1, replica_groups=mesh['mp'=4,'fsdp'=16,'dp'=4] {'fsdp'}, dimensions={1}, use_global_device_ids=true | all-gather | bytes 104448 | tf_op jit(solution)/shard_map/all_gather | solution.py:73
  41.7 2.1 fusion.105
  43.8 2.6 copy-done
  46.4 0.8 multiply_reduce_fusion.2
  47.2 0.1 slice_add_fusion.1
  47.3 25.2 %all-gather.7.cloned.1.call-done = bf16[1,3072,768]{2,1,0:T(8,128)(2,1)} async-done(((bf16[1,192,768]{2,1,0:T(8,128)(2,1)}), bf16[1,3072,768]{2,1,0:T(8,128)(2,1)}) %all-gather.7.cloned.1.call-update) | async-done | bytes 4718608 | tf_op jit(solution)/shard_map/all_gather | solution.py:79
  72.5 7.9 %fusion.38 = f32[512,64]{1,0:T(8,128)S(1)} fusion(f32[512,3072]{1,0:T(8,128)} %copy-done, s32[]{:T(128)S(6)} %select_n.2, bf16[1,3072,768]{2,1,0:T(8,128)(2,1)} %all-gather.7.cloned.1.call-done, bf16[3,64,768]{2,1,0:T(8,128)(2,1)S(1)} %copy-done.6, f32[3072]{0:T(1024)S(1)} %bitcast.103, f32[3072]{0:T(1024)S(1)} %bitcast.105, f32[512]{0:T(512)S(1)} %add_rsqrt_fusion.2, ...), kind=kOutput, calls=%fused_computation.36 | convolution fusion | flops 2474901504 | bytes 12840964 | tf_op jit(solution)/shard_map/dot_general | solution.py:39
  80.3 0.8 reshape.200
  81.2 0.7 all-gather.9.cloned.1.call-update
  81.9 0.5 all-gather.11.cloned.1.call-update
  82.4 0.2 all-reduce.9.cloned.1.call-start
  82.7 38.7 %all-reduce.5.cloned.1.call-done = f32[256,128]{1,0:T(8,128)} async-done(((f32[256,128]{1,0:T(8,128)}), f32[256,128]{1,0:T(8,128)}) %all-reduce.5.cloned.1.call-update) | async-done | bytes 131088 | tf_op jit(solution)/shard_map/psum | solution.py:82
  121.4 0.9 fusion.85
  122.3 0.1 convert_element_type.120
  122.4 1.0 fusion.106
  123.4 2.7 copy-done.2
  126.1 0.8 multiply_reduce_fusion.1
  126.9 56.7 %all-gather.9.cloned.1.call-done = bf16[1,3072,768]{2,1,0:T(8,128)(2,1)} async-done(((bf16[1,192,768]{2,1,0:T(8,128)(2,1)}), bf16[1,3072,768]{2,1,0:T(8,128)(2,1)}) %all-gather.9.cloned.1.call-update) | async-done | bytes 4718608 | tf_op jit(solution)/shard_map/all_gather | solution.py:94
  183.6 7.9 %fusion.46 = bf16[512,64]{0,1:T(8,128)(2,1)S(1)} fusion(f32[512,3072]{1,0:T(8,128)} %copy-done.2, s32[]{:T(128)S(6)} %select_n.2, bf16[1,3072,768]{2,1,0:T(8,128)(2,1)} %all-gather.9.cloned.1.call-done, f32[3072]{0:T(1024)S(1)} %bitcast.111, f32[3072]{0:T(1024)S(1)} %bitcast.112, f32[512]{0:T(512)S(1)} %add_rsqrt_fusion.1, ...), kind=kOutput, calls=%fused_computation.39 | convolution fusion | flops 2474934272 | bytes 12775428 | tf_op jit(solution)/shard_map/dot_general | solution.py:39
  191.5 0.1 copy.12
  191.6 0.8 convert_element_type.124
  192.4 1.0 fusion.107
  193.4 2.7 copy-done.1
  196.1 0.8 multiply_reduce_fusion
  196.8 48.7 %all-gather.11.cloned.1.call-done = bf16[1,3072,768]{2,1,0:T(8,128)(2,1)} async-done(((bf16[1,192,768]{2,1,0:T(8,128)(2,1)}), bf16[1,3072,768]{2,1,0:T(8,128)(2,1)}) %all-gather.11.cloned.1.call-update) | async-done | bytes 4718608 | tf_op jit(solution)/shard_map/all_gather | solution.py:93
  245.5 7.9 %fusion.40 = bf16[512,64]{0,1:T(8,128)(2,1)S(1)} fusion(f32[512,3072]{1,0:T(8,128)} %copy-done.1, s32[]{:T(128)S(6)} %select_n.2, bf16[1,3072,768]{2,1,0:T(8,128)(2,1)} %all-gather.11.cloned.1.call-done, f32[3072]{0:T(1024)S(1)} %bitcast.109, f32[3072]{0:T(1024)S(1)} %bitcast.110, f32[512]{0:T(512)S(1)} %add_rsqrt_fusion, ...), kind=kOutput, calls=%fused_computation.37 | convolution fusion | flops 2474934272 | bytes 12775428 | tf_op jit(solution)/shard_map/dot_general | solution.py:39
  253.4 0.1 copy.14
  253.5 0.8 convert_element_type.134
  254.3 7.9 %fusion.43 = bf16[512,64]{0,1:T(8,128)(2,1)S(1)} fusion(f32[512,3072]{1,0:T(8,128)} %copy-done.1, s32[]{:T(128)S(6)} %select_n.2, bf16[1,3072,768]{2,1,0:T(8,128)(2,1)} %all-gather.11.cloned.1.call-done, f32[3072]{0:T(1024)S(1)} %bitcast.108, f32[3072]{0:T(1024)S(1)} %bitcast.107, f32[512]{0:T(512)S(1)} %add_rsqrt_fusion, ...), kind=kOutput, calls=%fused_computation.38 | convolution fusion | flops 2474934272 | bytes 12775428 | tf_op jit(solution)/shard_map/dot_general | solution.py:39
  262.2 0.1 copy.13
  262.4 0.8 convert_element_type.129
  263.2 40.5 %all-reduce.9.cloned.1.call-done = (bf16[256,128]{1,0:T(8,128)(2,1)}, bf16[256,128]{1,0:T(8,128)(2,1)}, bf16[256,128]{1,0:T(8,128)(2,1)}) async-done(((bf16[256,128]{1,0:T(8,128)(2,1)}, bf16[256,128]{1,0:T(8,128)(2,1)}, bf16[256,128]{1,0:T(8,128)(2,1)}), (bf16[256,128]{1,0:T(8,128)(2,1)}, bf16[256,128]{1,0:T(8,128)(2,1)}, bf16[256,128]{1,0:T(8,128)(2,1)})) %all-reduce.9.cloned.1.call-update) | async-done | bytes 196624 | tf_op jit(solution)/shard_map/psum | solution.py:114
  303.7 1.5 abs_reduce_fusion
  305.2 37.2 %psum.46 = f32[]{:T(128)} all-reduce(f32[]{:T(128)} %abs_reduce_fusion), channel_id=1, replica_groups=mesh['mp'=4,'fsdp'=16,'dp'=4] {'fsdp'}, use_global_device_ids=true, to_apply=%region_11.12 | all-reduce | flops 1 | bytes 8 | tf_op jit(solution)/shard_map/psum | solution.py:124
  343.1 1.6 multiply_convert_fusion
  344.7 0.1 reshape.201
  344.8 8.2 %convolution_convert_fusion = bf16[3072,768]{1,0:T(8,128)(2,1)} fusion(bf16[512,64]{1,0:T(8,128)(2,1)S(1)} %reshape.201, bf16[3,64,768]{2,1,0:T(8,128)(2,1)S(1)} %copy-done.6, f32[512,3072]{1,0:T(8,128)} %copy-done, f32[3072]{0:T(1024)S(1)} %bitcast.104, f32[3072]{0:T(1024)S(1)} %bitcast.106, f32[512]{0:T(512)S(1)} %add_rsqrt_fusion.2, ...), kind=kOutput, calls=%fused_computation.7 | convolution fusion | flops 2476867584 | bytes 11268096 | tf_op jit(solution)/shard_map/dot_general | solution.py:133
  353.1 82.9 %reduce-scatter.2.cloned.1.call-done = bf16[192,768]{1,0:T(8,128)(2,1)} async-done(((bf16[3072,768]{1,0:T(8,128)(2,1)}), bf16[192,768]{1,0:T(8,128)(2,1)}) %reduce-scatter.2.cloned.1.call-update) | async-done | bytes 294928 | tf_op jit(solution)/shard_map/reduce_scatter | solution.py:132
  436.0 53.8 %all-reduce.7.cloned.1.call-done = bf16[192,768]{1,0:T(8,128)(2,1)} async-done(((bf16[192,768]{1,0:T(8,128)(2,1)}), bf16[192,768]{1,0:T(8,128)(2,1)}) %all-reduce.7.cloned.1.call-update) | async-done | bytes 294928 | tf_op jit(solution)/shard_map/psum | solution.py:140
  489.8 1.8 convert_element_type.139
  (36 shorter events, 0.6 us)
Async XLA Ops:
  7.2 65.3 %all-gather.7.cloned.1.call-start = ((), (), s32[]{:S(2)}) async-start(), calls=%async_computation.4 | async-start | bytes 5013504 | tf_op jit(solution)/shard_map/all_gather | solution.py:79
  9.3 112.0 %all-reduce.5.cloned.1.call-start = ((), (), s32[]{:S(2)}) async-start(), calls=%async_computation.1 | async-start | bytes 262144 | tf_op jit(solution)/shard_map/psum | solution.py:82
  41.7 30.8 %copy-start.6 = (bf16[3,64,768]{2,1,0:T(8,128)(2,1)S(1)}, bf16[3,64,768]{2,1,0:T(8,128)(2,1)}, u32[]{:S(2)}) copy-start(bf16[3,64,768]{2,1,0:T(8,128)(2,1)} %param.17) | copy-start | bytes 884740
  43.7 2.7 copy-start
  72.5 48.9 %copy-start.4 = (f32[1,256,128]{2,1,0:T(8,128)S(1)}, f32[1,256,128]{2,1,0:T(8,128)}, u32[]{:S(2)}) copy-start(f32[1,256,128]{2,1,0:T(8,128)} %param.10) | copy-start | bytes 393220
  72.5 49.9 %copy-start.3 = (bf16[3,64,3072]{2,1,0:T(8,128)(2,1)S(1)}, bf16[3,64,3072]{2,1,0:T(8,128)(2,1)}, u32[]{:S(2)}) copy-start(bf16[3,64,3072]{2,1,0:T(8,128)(2,1)} %param.14) | copy-start | bytes 3538948
  81.1 102.4 %all-gather.9.cloned.1.call-start = ((), (), s32[]{:S(2)}) async-start(), calls=%async_computation.5 | async-start | bytes 5013504 | tf_op jit(solution)/shard_map/all_gather | solution.py:94
  81.8 163.7 %all-gather.11.cloned.1.call-start = ((), (), s32[]{:S(2)}) async-start(), calls=%async_computation.6 | async-start | bytes 5013504 | tf_op jit(solution)/shard_map/all_gather | solution.py:93
  82.4 221.2 %all-reduce.9.cloned.1.call-start = ((), (), s32[]{:S(2)}) async-start(), calls=%async_computation.7 | async-start | bytes 393216 | tf_op jit(solution)/shard_map/psum | solution.py:114
  123.4 2.7 copy-start.2
  193.4 2.7 copy-start.1
  254.3 49.4 %copy-start.5 = (f32[256,128]{1,0:T(8,128)S(1)}, f32[256,128]{1,0:T(8,128)}, u32[]{:S(2)}) copy-start(f32[256,128]{1,0:T(8,128)} %all-reduce.5.cloned.1.call-done) | copy-start | bytes 393220
  263.1 172.8 %reduce-scatter.2.cloned.1.call-start = ((), (), s32[]{:S(2)}) async-start(), calls=%async_computation.2 | async-start | bytes 5013504 | tf_op jit(solution)/shard_map/reduce_scatter | solution.py:132
  353.0 136.8 %all-reduce.7.cloned.1.call-start = ((), (), s32[]{:S(2)}) async-start(), calls=%async_computation.3 | async-start | bytes 589824 | tf_op jit(solution)/shard_map/psum | solution.py:140
Sparse Core Ops, SparseCore 0:
  10.4 61.9 all-gather.6
  81.2 40.0 all-reduce.4
  124.1 59.4 all-gather.8
  186.7 58.7 all-gather.10
  263.3 40.3 all-reduce.8
  353.2 82.7 reduce-scatter.1
  438.6 51.1 all-reduce.6
where the time goes:
time: 499 us; the launch traced here: 498 us
  waiting for transfers between devices  348 us (70%)
  blocking collectives  60.9 us (12%)
  matrix products  49.3 us (10%)
  between operations  16.3 us (3%)
  local copies, waits for them, and re-layouts  13.7 us (3%)
  other arithmetic  10.1 us (2%)
    reduce_scatter x1, waiting for transfers between devices, body(): lax.psum_scatter(lax.dot_general(gen_hidden, upstream, (((0,), (0,)), (()...  82.9 us
    all_gather x1, waiting for transfers between devices, body(): lax.all_gather(proj_weight[2], 'fsdp', axis=0, tiled=True)  56.7 us
    psum x1, waiting for transfers between devices, body(): gen_grad = lax.psum(row_terms, 'dp').astype(jnp.float32)  53.8 us
    all_gather x1, waiting for transfers between devices, body(): lax.all_gather(proj_weight[1], 'fsdp', axis=0, tiled=True)  48.7 us
    psum x1, waiting for transfers between devices, body(): lax.psum(unembed_part(fake_cols + fake_part, unembed[2]).reshape(-1, 2 *...  40.5 us
    psum x1, waiting for transfers between devices, body(): clean_lat = lax.psum(clean_part, 'mp')  38.7 us
    psum x1, blocking collectives, body(): gap_total = lax.psum(jnp.sum(jnp.abs(clean_lat - real_pred)), 'fsdp')  37.2 us
    dot_general x4, matrix products, unembed_part(): lax.dot_general(residual_sum.astype(jnp.bfloat16), out_weight, (((1,), (1...  31.6 us
  transfers between devices with their start and end apart: 7, of which 7 were waited for; matrix products, arithmetic and copies ran while one was open for 5% of the time, Pallas kernels for 0%

commit v1 on v0

--- a/solution.py
+++ b/solution.py
@@ -51,6 +51,16 @@
 def body(
     gen_noise, renoise, gen_step, renoise_step, text_pooled, embed, mod_weight, proj_weight, unembed
 ):
+
+    def skins_scan(field, row_axis, in_dim):
+        tray = []
+        for _ in range(lax.axis_size(row_axis)):
+            tray.append(field)
+        clean = jnp.concatenate(tray, in_dim)
+        return lax.all_to_all(
+            clean, axis_name=row_axis, split_axis=in_dim, concat_axis=in_dim, tiled=True
+        )
+
     quarter = proj_weight.shape[2]
     col_start = lax.axis_index("mp") * quarter
     blank_text = jnp.zeros_like(text_pooled)
@@ -90,7 +100,7 @@
     fake_in = jnp.dot(noisy_bf, embed[2], preferred_element_type=jnp.float32)
     fake_hidden = modulate(normalize(fake_in), modulation[3])
     pieces = (
-        lax.all_gather(proj_weight[1], "fsdp", axis=0, tiled=True),
+        skins_scan(proj_weight[1], "fsdp", 0),
         lax.all_gather(proj_weight[2], "fsdp", axis=0, tiled=True),
     )
     cond_part = row_product(cond_hidden, pieces[0])

time: 499 us -> 465 us (0.932)
  waiting for transfers between devices: 348 us -> 306 us
  starting transfers between devices: 0.46 us -> 6.27 us
    all_gather x1 -> x0, waiting for transfers between devices: 48.7 us -> none  [body(): lax.all_gather(proj_weight[1], 'fsdp', axis=0, tiled=True)]
    all_gather x1, waiting for transfers between devices: 56.7 us -> 70.8 us  [body(): lax.all_gather(proj_weight[2], 'fsdp', axis=0, tiled=True)]
    psum x1, waiting for transfers between devices: 38.7 us -> 31.3 us  [body(): clean_lat = lax.psum(clean_part, 'mp')]
    all_to_all x0 -> x1, starting transfers between devices: none -> 5.85 us  [skins_scan(): lax.all_to_all(clean, axis_name=row_axis, split_axis=in_dim, concat_axis=...]
    unnamed x14 -> x33, local copies, waits for them, and re-layouts: 7.98 us -> 10.4 us
  transfers between devices with their start and end apart: 7 -> 7, of which waited for: 7 -> 6; matrix products, arithmetic and copies ran while one was open for 5% -> 5% of each run, Pallas kernels for 0% -> 0%
where the time goes in v1:
time: 465 us; the launch traced here: 464 us
  waiting for transfers between devices  306 us (66%)
  blocking collectives  60.9 us (13%)
  matrix products  48.3 us (10%)
  between operations  16.5 us (4%)
  local copies, waits for them, and re-layouts  16.1 us (3%)
  other arithmetic  10.1 us (2%)
  starting transfers between devices  6.27 us (1%)
    reduce_scatter x1, waiting for transfers between devices, body(): lax.psum_scatter(lax.dot_general(gen_hidden, upstream, (((0,), (0,)), (()...  82.7 us
    all_gather x1, waiting for transfers between devices, body(): lax.all_gather(proj_weight[2], 'fsdp', axis=0, tiled=True)  70.8 us
    psum x1, waiting for transfers between devices, body(): gen_grad = lax.psum(row_terms, 'dp').astype(jnp.float32)  53.7 us
    psum x1, waiting for transfers between devices, body(): lax.psum(unembed_part(fake_cols + fake_part, unembed[2]).reshape(-1, 2 *...  40.5 us
    psum x1, blocking collectives, body(): gap_total = lax.psum(jnp.sum(jnp.abs(clean_lat - real_pred)), 'fsdp')  37.2 us
    dot_general x4, matrix products, unembed_part(): lax.dot_general(residual_sum.astype(jnp.bfloat16), out_weight, (((1,), (1...  31.7 us
    psum x1, waiting for transfers between devices, body(): clean_lat = lax.psum(clean_part, 'mp')  31.3 us
    all_gather x1, waiting for transfers between devices, body(): lax.all_gather(proj_weight[0], 'fsdp', axis=0, tiled=True)  26.3 us
  transfers between devices with their start and end apart: 7, of which 6 were waited for; matrix products, arithmetic and copies ran while one was open for 5% of the time, Pallas kernels for 0%

profile of v1, /device:TPU:2, one launch (start us, length us, event | category | flops | bytes accessed | tf_op | source)
XLA Modules:
  0.0 464.2 jit_solution(14477814216234139560)
XLA Ops:
  7.2 2.0 fusion.90
  9.3 0.9 convert_element_type.109
  10.2 0.1 convert_element_type.110
  11.7 0.7 convert_reduce_fusion
  12.5 1.3 fusion.35
  13.8 1.3 fusion.39
  15.2 1.3 fusion.37
  16.5 1.3 fusion.41
  17.9 23.7 %all_gather.9 = f32[4,6144]{1,0:T(4,128)S(1)} all-gather(f32[4,384]{1,0:T(4,128)S(1)} %pad_maximum_fusion), channel_id=1, replica_groups=mesh['mp'=4,'fsdp'=16,'dp'=4] {'fsdp'}, dimensions={1}, use_global_device_ids=true | all-gather | bytes 104448 | tf_op jit(solution)/shard_map/all_gather | solution.py:83
  41.6 1.0 fusion.91
  42.7 2.6 copy-done
  45.3 0.8 multiply_reduce_fusion.2
  46.1 0.1 slice_add_fusion.1
  46.2 26.3 %all-gather.5.cloned.1.call-done = bf16[1,3072,768]{2,1,0:T(8,128)(2,1)} async-done(((bf16[1,192,768]{2,1,0:T(8,128)(2,1)}), bf16[1,3072,768]{2,1,0:T(8,128)(2,1)}) %all-gather.5.cloned.1.call-update) | async-done | bytes 4718608 | tf_op jit(solution)/shard_map/all_gather | solution.py:89
  72.5 7.8 %fusion.28 = f32[512,64]{1,0:T(8,128)S(1)} fusion(f32[512,3072]{1,0:T(8,128)} %copy-done, s32[]{:T(128)S(6)} %select_n.2, bf16[1,3072,768]{2,1,0:T(8,128)(2,1)} %all-gather.5.cloned.1.call-done, bf16[3,64,768]{2,1,0:T(8,128)(2,1)S(1)} %copy-done.8, f32[3072]{0:T(1024)S(1)} %bitcast.108, f32[3072]{0:T(1024)S(1)} %bitcast.110, f32[512]{0:T(512)S(1)} %add_rsqrt_fusion.2, ...), kind=kOutput, calls=%fused_computation.34 | convolution fusion | flops 2474901504 | bytes 12840964 | tf_op jit(solution)/shard_map/dot_general | solution.py:39
  80.3 0.8 reshape.202
  81.2 0.7 all-gather.7.cloned.1.call-update
  82.4 2.1 copy-done.4
  84.5 5.9 %all-to-all-start = ((bf16[16,192,768]{2,1,0:T(8,128)(2,1)}), bf16[16,192,768]{2,1,0:T(8,128)(2,1)}, u32[]{:S(2)}, u32[]{:S(2)}) async-start(bf16[16,192,768]{2,1,0:T(8,128)(2,1)} %bitcast.106), calls=%async_computation | async-start | bytes 9437184 | tf_op jit(solution)/shard_map/all_to_all | solution.py:60
  90.4 0.2 all-reduce.9.cloned.1.call-start
  90.6 31.3 %all-reduce.5.cloned.1.call-done = f32[256,128]{1,0:T(8,128)} async-done(((f32[256,128]{1,0:T(8,128)}), f32[256,128]{1,0:T(8,128)}) %all-reduce.5.cloned.1.call-update) | async-done | bytes 131088 | tf_op jit(solution)/shard_map/psum | solution.py:92
  121.9 0.9 fusion.71
  122.8 0.1 convert_element_type.120
  122.9 1.0 fusion.92
  123.9 2.7 copy-done.2
  126.6 0.8 multiply_reduce_fusion.1
  127.4 70.8 %all-gather.7.cloned.1.call-done = bf16[1,3072,768]{2,1,0:T(8,128)(2,1)} async-done(((bf16[1,192,768]{2,1,0:T(8,128)(2,1)}), bf16[1,3072,768]{2,1,0:T(8,128)(2,1)}) %all-gather.7.cloned.1.call-update) | async-done | bytes 4718608 | tf_op jit(solution)/shard_map/all_gather | solution.py:104
  198.1 8.0 %fusion.32 = bf16[512,64]{0,1:T(8,128)(2,1)S(1)} fusion(f32[512,3072]{1,0:T(8,128)} %copy-done.2, s32[]{:T(128)S(6)} %select_n.2, bf16[1,3072,768]{2,1,0:T(8,128)(2,1)} %all-gather.7.cloned.1.call-done, f32[3072]{0:T(1024)S(1)} %bitcast.116, f32[3072]{0:T(1024)S(1)} %bitcast.117, f32[512]{0:T(512)S(1)} %add_rsqrt_fusion.1, ...), kind=kOutput, calls=%fused_computation.37 | convolution fusion | flops 2474934272 | bytes 12775428 | tf_op jit(solution)/shard_map/dot_general | solution.py:39
  206.2 0.1 copy.12
  206.3 0.8 convert_element_type.124
  207.0 1.0 fusion.93
  208.1 2.7 copy-done.1
  210.7 0.8 multiply_reduce_fusion
  211.5 7.9 %fusion.30 = bf16[512,64]{0,1:T(8,128)(2,1)S(1)} fusion(f32[512,3072]{1,0:T(8,128)} %copy-done.1, s32[]{:T(128)S(6)} %select_n.2, bf16[3072,768]{1,0:T(8,128)(2,1)} %bitcast.22, f32[3072]{0:T(1024)S(1)} %bitcast.114, f32[3072]{0:T(1024)S(1)} %bitcast.115, f32[512]{0:T(512)S(1)} %add_rsqrt_fusion, f32[512]{0:T(512)S(1)} %broadcast_multiply_fusion, ...), kind=kOutput, calls=%fused_computation.35 | convolution fusion | flops 2474934272 | bytes 12775428 | tf_op jit(solution)/shard_map/dot_general | solution.py:39
  219.4 0.1 copy.14
  219.6 0.8 convert_element_type.134
  220.3 7.9 %fusion.31 = bf16[512,64]{0,1:T(8,128)(2,1)S(1)} fusion(f32[512,3072]{1,0:T(8,128)} %copy-done.1, s32[]{:T(128)S(6)} %select_n.2, bf16[3072,768]{1,0:T(8,128)(2,1)} %bitcast.22, f32[3072]{0:T(1024)S(1)} %bitcast.113, f32[3072]{0:T(1024)S(1)} %bitcast.112, f32[512]{0:T(512)S(1)} %add_rsqrt_fusion, f32[512]{0:T(512)S(1)} %broadcast_multiply_fusion, ...), kind=kOutput, calls=%fused_computation.36 | convolution fusion | flops 2474934272 | bytes 12775428 | tf_op jit(solution)/shard_map/dot_general | solution.py:39
  228.3 0.1 copy.13
  228.4 0.7 convert_element_type.129
  229.2 40.5 %all-reduce.9.cloned.1.call-done = (bf16[256,128]{1,0:T(8,128)(2,1)}, bf16[256,128]{1,0:T(8,128)(2,1)}, bf16[256,128]{1,0:T(8,128)(2,1)}) async-done(((bf16[256,128]{1,0:T(8,128)(2,1)}, bf16[256,128]{1,0:T(8,128)(2,1)}, bf16[256,128]{1,0:T(8,128)(2,1)}), (bf16[256,128]{1,0:T(8,128)(2,1)}, bf16[256,128]{1,0:T(8,128)(2,1)}, bf16[256,128]{1,0:T(8,128)(2,1)})) %all-reduce.9.cloned.1.call-update) | async-done | bytes 196624 | tf_op jit(solution)/shard_map/psum | solution.py:124
  269.7 1.5 abs_reduce_fusion
  271.2 37.2 %psum.46 = f32[]{:T(128)} all-reduce(f32[]{:T(128)} %abs_reduce_fusion), channel_id=1, replica_groups=mesh['mp'=4,'fsdp'=16,'dp'=4] {'fsdp'}, use_global_device_ids=true, to_apply=%region_11.12 | all-reduce | flops 1 | bytes 8 | tf_op jit(solution)/shard_map/psum | solution.py:134
  309.1 1.6 multiply_convert_fusion
  310.7 0.1 reshape.203
  310.8 8.2 %convolution_convert_fusion = bf16[3072,768]{1,0:T(8,128)(2,1)} fusion(bf16[512,64]{1,0:T(8,128)(2,1)S(1)} %reshape.203, bf16[3,64,768]{2,1,0:T(8,128)(2,1)S(1)} %copy-done.8, f32[512,3072]{1,0:T(8,128)} %copy-done, f32[3072]{0:T(1024)S(1)} %bitcast.109, f32[3072]{0:T(1024)S(1)} %bitcast.111, f32[512]{0:T(512)S(1)} %add_rsqrt_fusion.2, ...), kind=kOutput, calls=%fused_computation.7 | convolution fusion | flops 2476867584 | bytes 11268096 | tf_op jit(solution)/shard_map/dot_general | solution.py:143
  319.1 82.7 %reduce-scatter.2.cloned.1.call-done = bf16[192,768]{1,0:T(8,128)(2,1)} async-done(((bf16[3072,768]{1,0:T(8,128)(2,1)}), bf16[192,768]{1,0:T(8,128)(2,1)}) %reduce-scatter.2.cloned.1.call-update) | async-done | bytes 294928 | tf_op jit(solution)/shard_map/reduce_scatter | solution.py:142
  401.8 53.7 %all-reduce.7.cloned.1.call-done = bf16[192,768]{1,0:T(8,128)(2,1)} async-done(((bf16[192,768]{1,0:T(8,128)(2,1)}), bf16[192,768]{1,0:T(8,128)(2,1)}) %all-reduce.7.cloned.1.call-update) | async-done | bytes 294928 | tf_op jit(solution)/shard_map/psum | solution.py:150
  455.5 1.8 convert_element_type.139
  (55 shorter events, 0.9 us)
Async XLA Ops:
  7.2 34.4 %copy-start.5 = (bf16[3,64,3072]{2,1,0:T(8,128)(2,1)S(1)}, bf16[3,64,3072]{2,1,0:T(8,128)(2,1)}, u32[]{:S(2)}) copy-start(bf16[3,64,3072]{2,1,0:T(8,128)(2,1)} %param.14) | copy-start | bytes 3538948
  7.2 65.3 %all-gather.5.cloned.1.call-start = ((), (), s32[]{:S(2)}) async-start(), calls=%async_computation.5 | async-start | bytes 5013504 | tf_op jit(solution)/shard_map/all_gather | solution.py:89
  9.2 112.6 %all-reduce.5.cloned.1.call-start = ((), (), s32[]{:S(2)}) async-start(), calls=%async_computation.2 | async-start | bytes 262144 | tf_op jit(solution)/shard_map/psum | solution.py:92
  42.7 2.7 copy-start
  42.7 29.9 %copy-start.8 = (bf16[3,64,768]{2,1,0:T(8,128)(2,1)S(1)}, bf16[3,64,768]{2,1,0:T(8,128)(2,1)}, u32[]{:S(2)}) copy-start(bf16[3,64,768]{2,1,0:T(8,128)(2,1)} %param.17) | copy-start | bytes 884740
  72.5 9.4 %copy-start.3 = (bf16[3,192,768]{2,1,0:T(8,128)(2,1)S(1)}, bf16[3,192,768]{2,1,0:T(8,128)(2,1)}, u32[]{:S(2)}) copy-start(bf16[3,192,768]{2,1,0:T(8,128)(2,1)} %param.16) | copy-start | bytes 2654212
  81.1 117.0 %all-gather.7.cloned.1.call-start = ((), (), s32[]{:S(2)}) async-start(), calls=%async_computation.6 | async-start | bytes 5013504 | tf_op jit(solution)/shard_map/all_gather | solution.py:104
  82.4 2.1 copy-start.4
  84.5 37.4 %copy-start.6 = (f32[1,256,128]{2,1,0:T(8,128)S(1)}, f32[1,256,128]{2,1,0:T(8,128)}, u32[]{:S(2)}) copy-start(f32[1,256,128]{2,1,0:T(8,128)} %param.10) | copy-start | bytes 393220
  84.5 127.0 %all-to-all-start = ((bf16[16,192,768]{2,1,0:T(8,128)(2,1)}), bf16[16,192,768]{2,1,0:T(8,128)(2,1)}, u32[]{:S(2)}, u32[]{:S(2)}) async-start(bf16[16,192,768]{2,1,0:T(8,128)(2,1)} %bitcast.106), calls=%async_computation | async-start | bytes 9437184 | tf_op jit(solution)/shard_map/all_to_all | solution.py:60
  90.4 179.3 %all-reduce.9.cloned.1.call-start = ((), (), s32[]{:S(2)}) async-start(), calls=%async_computation.7 | async-start | bytes 393216 | tf_op jit(solution)/shard_map/psum | solution.py:124
  123.9 2.7 copy-start.2
  208.1 2.7 copy-start.1
  220.3 49.4 %copy-start.7 = (f32[256,128]{1,0:T(8,128)S(1)}, f32[256,128]{1,0:T(8,128)}, u32[]{:S(2)}) copy-start(f32[256,128]{1,0:T(8,128)} %all-reduce.5.cloned.1.call-done) | copy-start | bytes 393220
  229.1 172.7 %reduce-scatter.2.cloned.1.call-start = ((), (), s32[]{:S(2)}) async-start(), calls=%async_computation.3 | async-start | bytes 5013504 | tf_op jit(solution)/shard_map/reduce_scatter | solution.py:142
  319.1 136.5 %all-reduce.7.cloned.1.call-start = ((), (), s32[]{:S(2)}) async-start(), calls=%async_computation.4 | async-start | bytes 589824 | tf_op jit(solution)/shard_map/psum | solution.py:150
Sparse Core Ops, SparseCore 0:
  10.4 62.0 all-gather.4
  81.3 40.5 all-reduce.4
  125.2 72.9 all-gather.6
  229.3 40.3 all-reduce.8
  319.2 82.5 reduce-scatter.1
  404.3 51.1 all-reduce.6
